TPU v7x, 128 devices: a whole 4x4x4 slice. The times are simulated.
128 devices in a mesh: dp: 4 (over y_lo, core), seq: 32 (over x, y_hi, z).
Axes of the slice: x: 4, y: 4 (y_hi: 2, y_lo: 2; y = y_hi * 2 + y_lo), z: 4, core: 2. Of those that a mesh axis runs over, the one named last changes fastest.
Arguments:
- tokens: bfloat16 [4, 16384, 2048], P('dp', 'seq'), may hold values from -5 to 5, as said below
- gain_first: float32 [2048], replicated, may hold values from 0.25 to 1.75
- inputs_first: bfloat16 [2048, 3072], P(('dp', 'seq')), may hold values from -1 to 1, as said below
- output_first: bfloat16 [1024, 2048], P(('dp', 'seq')), may hold values from -0.5 to 0.5
- gain_second: float32 [2048], replicated, may hold values from 0.25 to 1.75
- inputs_second: bfloat16 [2048, 3072], P(('dp', 'seq')), may hold values from -1 to 1, as said below
- output_second: bfloat16 [1024, 2048], P(('dp', 'seq')), may hold values from -0.5 to 0.5
- starts: int32 [4, 32], P('dp'), may hold values from 0 to 32256, as said below
- band_edges: int32 [2], replicated, may hold values from 4 to 62, as said below
Outputs:
- layer_out: bfloat16 [4, 16384, 2048], P('dp', 'seq')
Inputs may be any that keep to these rules, and one draw needn't show every extreme that they name: `tokens`: entries are real-valued and lie within -5 to 5. `inputs_first`: entries lie within -6 / sqrt(2048) to 6 / sqrt(2048). `inputs_second`: entries lie within -6 / sqrt(2048) to 6 / sqrt(2048). `starts`: along a sequence each start exceeds the one before by 512 to 1024; the first is at most 512. band_edges[0] < band_edges[1], with at least 4 between them; band_edges[1] is 62.
All inputs are finite; a program needn't handle non-finite values.
Results may differ from a plain program's by a relative error of at most 0.025.
Values may be sent and summed in bfloat16 or wider, within the bound.
No kernel may reach another device: no remote copies, remote signals or barrier semaphores. Data moves between devices by JAX's collectives and lax.ppermute only.
A program may use at most 128 MiB of HBM per device.

v0:
```python
import math
import jax
import jax.numpy as jnp
from jax import lax
from jax.sharding import PartitionSpec as P

HEADS = 8
HEAD = 128
C = 512
SCALE = 8


def normed(values, gain):
    as_float = values.astype(jnp.float32)
    inv_rms = lax.rsqrt(jnp.mean(as_float * as_float, axis=-1, keepdims=True) + 1e-05)
    return (as_float * inv_rms * gain).astype(jnp.bfloat16)


def frequencies(band_edges, half_size):
    dim_index = jnp.arange(half_size, dtype=jnp.float32)
    base_freq = jnp.power(10000.0, -dim_index / half_size)
    lower_edge = band_edges[0].astype(jnp.float32)
    upper_edge = band_edges[1].astype(jnp.float32)
    ramp_share = jnp.clip((dim_index - lower_edge) / (upper_edge - lower_edge), 0.0, 1.0)
    return base_freq * (1.0 - ramp_share) + base_freq * ramp_share / SCALE


def rotary(projected, positions, frequency):
    half_size = frequency.shape[0]
    angles = positions.astype(jnp.float32)[..., None] * frequency
    mscale = 0.1 * math.log(SCALE) + 1.0
    cosine = (jnp.cos(angles) * mscale)[..., None, :]
    sine_part = (jnp.sin(angles) * mscale)[..., None, :]
    first_half = projected[..., :half_size]
    second_half = projected[..., half_size:]
    return jnp.concatenate(
        [
            first_half * cosine - second_half * sine_part,
            second_half * cosine + first_half * sine_part,
        ],
        axis=-1,
    ).astype(jnp.bfloat16)


def softmax_rows(scores):
    row_max = jnp.max(scores, axis=-1, keepdims=True)
    weights = jnp.exp(scores - row_max)
    return (weights / jnp.sum(weights, axis=-1, keepdims=True)).astype(jnp.bfloat16)


def attend_block(triple):
    queries, key_rows, values = triple
    length = queries.shape[0]
    scores = jnp.einsum(
        "qd,kd->qk", queries, key_rows, preferred_element_type=jnp.float32
    ) / math.sqrt(queries.shape[-1])
    causal = jnp.arange(length)[None, :] <= jnp.arange(length)[:, None]
    scores = jnp.where(causal, scores, -1e30)
    probability = softmax_rows(scores)
    return jnp.dot(probability, values, preferred_element_type=jnp.float32).astype(jnp.bfloat16)


def row_attention(queries, key_rows, values):
    grid_rows, row_len, head_count, head_size = queries.shape

    def flatten_heads(tensor):
        return tensor.transpose(0, 2, 1, 3).reshape(grid_rows * head_count, row_len, head_size)

    result = lax.map(
        attend_block, (flatten_heads(queries), flatten_heads(key_rows), flatten_heads(values))
    )
    return result.reshape(grid_rows, head_count, row_len, head_size).transpose(0, 2, 1, 3)


def column_attention(queries, key_rows, values):
    length = queries.shape[0]
    scores = jnp.einsum(
        "rchd,schd->chrs", queries, key_rows, preferred_element_type=jnp.float32
    ) / math.sqrt(queries.shape[-1])
    causal = jnp.arange(length)[None, :] <= jnp.arange(length)[:, None]
    scores = jnp.where(causal[None, None], scores, -1e30)
    probability = softmax_rows(scores)
    return jnp.einsum(
        "chrs,schd->rchd", probability, values, preferred_element_type=jnp.float32
    ).astype(jnp.bfloat16)


def columns_then_back(triple):
    attended = column_attention(triple[0], triple[1], triple[2])
    return lax.all_to_all(attended, "seq", split_axis=0, concat_axis=1, tiled=True)


def accumulate(hidden, block_rows):
    return jnp.dot(hidden, block_rows, preferred_element_type=jnp.float32)


def shards(
    tokens,
    gain_first,
    inputs_first,
    output_first,
    gain_second,
    inputs_second,
    output_second,
    starts,
    band_edges,
):
    residual = tokens[0]
    tok_count, model_width = residual.shape
    rows_dev = tok_count // C
    attn_width = HEADS * HEAD
    frequency = frequencies(band_edges, HEAD // 2)
    block_starts = starts[0]
    own_start = lax.dynamic_index_in_dim(block_starts, lax.axis_index("seq"), 0, keepdims=False)
    position_grid = (own_start + jnp.arange(tok_count, dtype=jnp.int32)).reshape(rows_dev, C)
    hidden = normed(residual, gain_first)
    group_rows = lax.all_gather(inputs_first, "seq", axis=0, tiled=True)
    projected = accumulate(hidden, lax.all_gather(group_rows, "dp", axis=0, tiled=True))
    projected = projected.reshape(rows_dev, C, 3, HEADS, HEAD)
    queries = rotary(projected[:, :, 0], position_grid, frequency)
    key_rows = rotary(projected[:, :, 1], position_grid, frequency)
    values = projected[:, :, 2].astype(jnp.bfloat16)
    attended = row_attention(queries, key_rows, values).reshape(tok_count, attn_width)
    group_rows = lax.all_gather(output_first, "seq", axis=0, tiled=True)
    branch = accumulate(attended, lax.all_gather(group_rows, "dp", axis=0, tiled=True))
    middle = (residual.astype(jnp.float32) + branch).astype(jnp.bfloat16)
    hidden = normed(middle, gain_second)
    second_rows = lax.all_gather(inputs_second, "seq", axis=0, tiled=True)
    projected = accumulate(hidden, lax.all_gather(second_rows, "dp", axis=0, tiled=True)).reshape(
        rows_dev, C, 3, HEADS, HEAD
    )
    queries = rotary(projected[:, :, 0], position_grid, frequency)
    key_rows = rotary(projected[:, :, 1], position_grid, frequency)
    values = projected[:, :, 2].astype(jnp.bfloat16)
    attended = columns_then_back(
        (
            lax.all_to_all(queries, "seq", split_axis=1, concat_axis=0, tiled=True),
            lax.all_to_all(key_rows, "seq", split_axis=1, concat_axis=0, tiled=True),
            lax.all_to_all(values, "seq", split_axis=1, concat_axis=0, tiled=True),
        )
    )
    attended = attended.reshape(tok_count, attn_width)
    group_rows = lax.all_gather(output_second, "seq", axis=0, tiled=True)
    branch = accumulate(attended, lax.all_gather(group_rows, "dp", axis=0, tiled=True))
    return (middle.astype(jnp.float32) + branch).astype(jnp.bfloat16)[None]


def solution(mesh):
    return jax.shard_map(
        shards,
        mesh=mesh,
        in_specs=(
            P("dp", "seq", None),
            P(),
            P(("dp", "seq"), None),
            P(("dp", "seq"), None),
            P(),
            P(("dp", "seq"), None),
            P(("dp", "seq"), None),
            P("dp", None),
            P(),
        ),
        out_specs=P("dp", "seq", None),
        check_vma=False,
    )
```

profile of v0, /device:TPU:0, one launch (start us, length us, event | category | flops | bytes accessed | tf_op | source)
XLA Modules:
  0.0 710.8 jit_solution(3117279610338200591)
XLA Ops:
  6.5 0.7 all-gather.9.cloned.1.call-update
  7.3 0.7 all-gather.13.cloned.1.call-update
  8.1 0.7 all-gather.17.cloned.1.call-update
  9.4 78.6 %all-gather.9.cloned.1.call-done = bf16[512,3072]{1,0:T(8,128)(2,1)} async-done(((bf16[16,3072]{1,0:T(8,128)(2,1)}), bf16[512,3072]{1,0:T(8,128)(2,1)}) %all-gather.9.cloned.1.call-update) | async-done | bytes 3145744 | tf_op jit(solution)/shard_map/all_gather | solution.py:117
  88.0 66.6 %all-gather.13.cloned.1.call-done = bf16[256,2048]{1,0:T(8,128)(2,1)} async-done(((bf16[8,2048]{1,0:T(8,128)(2,1)}), bf16[256,2048]{1,0:T(8,128)(2,1)}) %all-gather.13.cloned.1.call-update) | async-done | bytes 1048592 | tf_op jit(solution)/shard_map/all_gather | solution.py:124
  154.7 74.8 %all-gather.17.cloned.1.call-done = bf16[512,3072]{1,0:T(8,128)(2,1)} async-done(((bf16[16,3072]{1,0:T(8,128)(2,1)}), bf16[512,3072]{1,0:T(8,128)(2,1)}) %all-gather.17.cloned.1.call-update) | async-done | bytes 3145744 | tf_op jit(solution)/shard_map/all_gather | solution.py:128
  229.6 0.7 fusion.62
  231.7 0.7 constant_dynamic-slice_fusion
  232.3 0.7 add_convert_fusion.4
  233.6 0.5 fusion.45
  234.1 62.0 %all-gather.21.cloned.1.call-done = bf16[256,2048]{1,0:T(8,128)(2,1)} async-done(((bf16[8,2048]{1,0:T(8,128)(2,1)}), bf16[256,2048]{1,0:T(8,128)(2,1)}) %all-gather.21.cloned.1.call-update) | async-done | bytes 1048592 | tf_op jit(solution)/shard_map/all_gather | solution.py:143
  296.1 112.7 %all-gather.11.cloned.1.call-done = bf16[2048,3072]{1,0:T(8,128)(2,1)} async-done(((bf16[512,3072]{1,0:T(8,128)(2,1)}), bf16[2048,3072]{1,0:T(8,128)(2,1)}) %all-gather.11.cloned.1.call-update) | async-done | bytes 12582928 | tf_op jit(solution)/shard_map/all_gather | solution.py:118
  408.8 16.9 %copy.33 = bf16[3072,2048]{1,0:T(8,128)(2,1)} copy(bf16[3072,2048]{0,1:T(8,128)(2,1)} %bitcast.97) | data formatting | bytes 25165824 | tf_op jit(solution)/shard_map/dot_general | solution.py:94
  425.7 9.6 %convolution_bitcast_fusion = f32[1,512,3,8,128]{1,4,3,2,0:T(8,128)S(1)} fusion(bf16[3,8,128,2048]{3,2,1,0:T(8,128)(2,1)} %bitcast.98, bf16[1,512,2048]{2,1,0:T(8,128)(2,1)S(1)} %copy-done.3, f32[2048]{0:T(1024)S(1)} %copy-done.5, f32[512]{0:T(512)S(1)} %add_rsqrt_fusion.1), kind=kOutput, calls=%fused_computation.34 | convolution fusion | flops 6446645248 | bytes 20981760 | tf_op jit(solution)/shard_map/dot_general | solution.py:94
  435.8 1.1 fusion.33
  436.9 0.7 subtract_convert_fusion.2
  437.7 1.5 maximum_bitcast_fusion
  439.1 28.9 %while.10 = (s32[]{:T(128)}, bf16[8,512,128]{1,2,0:T(8,128)(2,1)}, bf16[8,512,128]{1,2,0:T(8,128)(2,1)}, bf16[8,512,128]{1,2,0:T(8,128)(2,1)}, bf16[8,512,128]{1,2,0:T(8,128)(2,1)}, /*index=5*/s32[]{:T(128)}) while((s32[]{:T(128)}, bf16[8,512,128]{1,2,0:T(8,128)(2,1)}, bf16[8,512,128]{1,2,0:T(8,128)(2,1)}, bf16[8,512,128]{1,2,0:T(8,128)(2,1)}, ...), condition=%wide.region_4.5_spmd, body=%wide.region_1.4_spmd.sunk | while | flops 136641536 | bytes 4206661 | solution.py:69
  439.1 1.3 fusion.78
  440.7 1.3 fusion.80
  442.1 0.7 constant_dynamic-update-slice_fusion.2
  442.8 1.3 fusion.78
  444.3 1.3 fusion.80
  445.7 0.7 constant_dynamic-update-slice_fusion.2
  446.4 1.3 fusion.78
  447.9 1.3 fusion.80
  449.3 0.7 constant_dynamic-update-slice_fusion.2
  450.0 1.3 fusion.78
  451.5 1.3 fusion.80
  452.9 0.7 constant_dynamic-update-slice_fusion.2
  453.6 1.3 fusion.78
  455.1 1.3 fusion.80
  456.5 0.7 constant_dynamic-update-slice_fusion.2
  457.2 1.3 fusion.78
  458.7 1.3 fusion.80
  460.1 0.7 constant_dynamic-update-slice_fusion.2
  460.8 1.3 fusion.78
  462.3 1.3 fusion.80
  463.7 0.7 constant_dynamic-update-slice_fusion.2
  464.4 1.3 fusion.78
  465.9 1.3 fusion.80
  467.3 0.7 constant_dynamic-update-slice_fusion.2
  468.0 6.6 fusion.18
  474.6 102.0 %all-gather.19.cloned.1.call-done = bf16[2048,3072]{1,0:T(8,128)(2,1)} async-done(((bf16[512,3072]{1,0:T(8,128)(2,1)}), bf16[2048,3072]{1,0:T(8,128)(2,1)}) %all-gather.19.cloned.1.call-update) | async-done | bytes 12582928 | tf_op jit(solution)/shard_map/all_gather | solution.py:129
  576.6 10.4 %fusion.23 = f32[512,3072]{0,1:T(8,128)S(1)} fusion(bf16[2048,3072]{1,0:T(8,128)(2,1)} %all-gather.19.cloned.1.call-done, bf16[512,2048]{1,0:T(8,128)(2,1)} %get-tuple-element.81, f32[2048]{0:T(1024)S(1)} %copy-done.6, f32[512]{0:T(512)S(1)} %add_rsqrt_fusion), kind=kOutput, calls=%fused_computation.35 | convolution fusion | flops 6446645248 | bytes 20981760 | tf_op jit(solution)/shard_map/dot_general | solution.py:94
  587.0 0.6 slice_bitcast_fusion.1
  587.7 2.0 copy-done.2
  589.7 0.7 subtract_convert_fusion.1
  590.5 1.5 copy.40
  592.0 9.8 %all-to-all-start.1 = ((bf16[1,512,8,128]{3,2,0,1:T(8,128)(2,1)}), bf16[1,512,8,128]{3,2,0,1:T(8,128)(2,1)S(1)}, u32[]{:S(2)}, u32[]{:S(2)}) async-start(bf16[1,512,8,128]{3,2,0,1:T(8,128)(2,1)} %copy.40), calls=%async_computation.1 | async-start | bytes 2097152 | tf_op jit(solution)/shard_map/all_to_all | solution.py:137
  601.9 1.5 copy.41
  603.4 19.6 %all-to-all-done.1 = bf16[1,512,8,128]{3,2,0,1:T(8,128)(2,1)S(1)} async-done(((bf16[1,512,8,128]{3,2,0,1:T(8,128)(2,1)}), bf16[1,512,8,128]{3,2,0,1:T(8,128)(2,1)S(1)}, u32[]{:S(2)}, u32[]{:S(2)}) %all-to-all-start.1) | async-done | bytes 1048608 | tf_op jit(solution)/shard_map/all_to_all | solution.py:137
  623.0 5.4 all-to-all-start.2
  628.3 1.7 fusion.34
  630.1 1.5 copy.39
  631.5 17.8 %all-to-all-done.2 = bf16[1,512,8,128]{3,2,0,1:T(8,128)(2,1)S(1)} async-done(((bf16[1,512,8,128]{3,2,0,1:T(8,128)(2,1)}), bf16[1,512,8,128]{3,2,0,1:T(8,128)(2,1)S(1)}, u32[]{:S(2)}, u32[]{:S(2)}) %all-to-all-start.2) | async-done | bytes 1048608 | tf_op jit(solution)/shard_map/all_to_all | solution.py:138
  649.3 4.7 all-to-all-start
  654.0 3.3 fusion.63
  657.3 14.7 %all-to-all-done = bf16[1,512,8,128]{3,2,0,1:T(8,128)(2,1)S(1)} async-done(((bf16[1,512,8,128]{3,2,0,1:T(8,128)(2,1)}), bf16[1,512,8,128]{3,2,0,1:T(8,128)(2,1)S(1)}, u32[]{:S(2)}, u32[]{:S(2)}) %all-to-all-start) | async-done | bytes 1048608 | tf_op jit(solution)/shard_map/all_to_all | solution.py:139
  672.0 2.6 fusion.32
  674.6 1.4 copy.46
  676.0 4.6 all-to-all-start.3
  680.6 17.5 %all-to-all-done.3 = bf16[32,16,8,128]{3,2,1,0:T(8,128)(2,1)S(1)} async-done(((bf16[32,16,8,128]{3,2,1,0:T(8,128)(2,1)}), bf16[32,16,8,128]{3,2,1,0:T(8,128)(2,1)S(1)}, u32[]{:S(2)}, u32[]{:S(2)}) %all-to-all-start.3) | async-done | bytes 1048608 | tf_op jit(solution)/shard_map/all_to_all | solution.py:90
  698.1 5.9 fusion.22
  (55 shorter events, 4.6 us)
Async XLA Ops:
  6.5 225.1 %copy-start = (s32[1,32]{1,0:T(1,128)S(1)}, s32[1,32]{1,0:T(1,128)}, u32[]{:S(2)}) copy-start(s32[1,32]{1,0:T(1,128)} %param.18) | copy-start | bytes 388
  6.5 81.4 %all-gather.9.cloned.1.call-start = ((), (), s32[]{:S(2)}) async-start(), calls=%async_computation.4 | async-start | bytes 3244032 | tf_op jit(solution)/shard_map/all_gather | solution.py:117
  7.3 147.4 %all-gather.13.cloned.1.call-start = ((), (), s32[]{:S(2)}) async-start(), calls=%async_computation.6 | async-start | bytes 1081344 | tf_op jit(solution)/shard_map/all_gather | solution.py:124
  8.0 221.5 %all-gather.17.cloned.1.call-start = ((), (), s32[]{:S(2)}) async-start(), calls=%async_computation.8 | async-start | bytes 3244032 | tf_op jit(solution)/shard_map/all_gather | solution.py:128
  8.7 287.3 %all-gather.21.cloned.1.call-start = ((), (), s32[]{:S(2)}) async-start(), calls=%async_computation.10 | async-start | bytes 1081344 | tf_op jit(solution)/shard_map/all_gather | solution.py:143
  9.3 399.5 %all-gather.11.cloned.1.call-start = ((), (), s32[]{:S(2)}) async-start(), calls=%async_computation.5 | async-start | bytes 15728640 | tf_op jit(solution)/shard_map/all_gather | solution.py:118
  88.0 380.0 %all-gather.15.cloned.1.call-start = ((), (), s32[]{:S(2)}) async-start(), calls=%async_computation.7 | async-start | bytes 5242880 | tf_op jit(solution)/shard_map/all_gather | solution.py:125
  154.6 75.0 %copy-start.4 = (s32[2]{0:T(128)S(1)}, s32[2]{0:T(128)}, u32[]{:S(2)}) copy-start(s32[2]{0:T(128)} %param.19) | copy-start | bytes 28
  154.6 78.4 %copy-start.3 = (bf16[1,512,2048]{2,1,0:T(8,128)(2,1)S(1)}, bf16[1,512,2048]{2,1,0:T(8,128)(2,1)}, u32[]{:S(2)}) copy-start(bf16[1,512,2048]{2,1,0:T(8,128)(2,1)} %param.11) | copy-start | bytes 6291460
  154.7 422.0 %all-gather.19.cloned.1.call-start = ((), (), s32[]{:S(2)}) async-start(), calls=%async_computation.9 | async-start | bytes 15728640 | tf_op jit(solution)/shard_map/all_gather | solution.py:129
  229.6 451.0 %all-gather.23.cloned.1.call-start = ((), (), s32[]{:S(2)}) async-start(), calls=%async_computation.11 | async-start | bytes 5242880 | tf_op jit(solution)/shard_map/all_gather | solution.py:144
  408.8 16.9 %copy-start.5 = (f32[2048]{0:T(1024)S(1)}, f32[2048]{0:T(1024)}, u32[]{:S(2)}) copy-start(f32[2048]{0:T(1024)} %param.12) | copy-start | bytes 24580
  468.0 108.6 %copy-start.6 = (f32[2048]{0:T(1024)S(1)}, f32[2048]{0:T(1024)}, u32[]{:S(2)}) copy-start(f32[2048]{0:T(1024)} %param.15) | copy-start | bytes 24580
  587.0 2.7 copy-start.2
  592.0 31.0 %all-to-all-start.1 = ((bf16[1,512,8,128]{3,2,0,1:T(8,128)(2,1)}), bf16[1,512,8,128]{3,2,0,1:T(8,128)(2,1)S(1)}, u32[]{:S(2)}, u32[]{:S(2)}) async-start(bf16[1,512,8,128]{3,2,0,1:T(8,128)(2,1)} %copy.40), calls=%async_computation.1 | async-start | bytes 2097152 | tf_op jit(solution)/shard_map/all_to_all | solution.py:137
  623.0 26.3 %all-to-all-start.2 = ((bf16[1,512,8,128]{3,2,0,1:T(8,128)(2,1)}), bf16[1,512,8,128]{3,2,0,1:T(8,128)(2,1)S(1)}, u32[]{:S(2)}, u32[]{:S(2)}) async-start(bf16[1,512,8,128]{3,2,0,1:T(8,128)(2,1)} %copy.41), calls=%async_computation.2 | async-start | bytes 2097152 | tf_op jit(solution)/shard_map/all_to_all | solution.py:138
  649.3 22.7 %all-to-all-start = ((bf16[1,512,8,128]{3,2,0,1:T(8,128)(2,1)}), bf16[1,512,8,128]{3,2,0,1:T(8,128)(2,1)S(1)}, u32[]{:S(2)}, u32[]{:S(2)}) async-start(bf16[1,512,8,128]{3,2,0,1:T(8,128)(2,1)} %copy.39), calls=%async_computation | async-start | bytes 2097152 | tf_op jit(solution)/shard_map/all_to_all | solution.py:139
  674.6 23.5 %copy-start.7 = (bf16[512,2048]{1,0:T(8,128)(2,1)S(1)}, bf16[512,2048]{1,0:T(8,128)(2,1)}, u32[]{:S(2)}) copy-start(bf16[512,2048]{1,0:T(8,128)(2,1)} %get-tuple-element.81) | copy-start | bytes 6291460
  676.0 22.1 %all-to-all-start.3 = ((bf16[32,16,8,128]{3,2,1,0:T(8,128)(2,1)}), bf16[32,16,8,128]{3,2,1,0:T(8,128)(2,1)S(1)}, u32[]{:S(2)}, u32[]{:S(2)}) async-start(bf16[32,16,8,128]{3,2,1,0:T(8,128)(2,1)} %copy.46), calls=%async_computation.3 | async-start | bytes 2097152 | tf_op jit(solution)/shard_map/all_to_all | solution.py:90
  698.1 5.9 copy-start.1
Sparse Core Ops, SparseCore 0:
  10.4 77.4 all-gather.8
  90.9 63.6 all-gather.12
  157.7 71.8 all-gather.16
  232.4 63.6 all-gather.20
  297.6 111.1 all-gather.10
  410.4 48.7 all-gather.14
  460.8 115.8 all-gather.18
  578.3 71.1 all-gather.22
where the time goes:
time: 712 us; the launch traced here: 711 us
  waiting for transfers between devices  569 us (80%)
  matrix products  59.2 us (8%)
  local copies, waits for them, and re-layouts  36.2 us (5%)
  starting transfers between devices  24.8 us (3%)
  between operations  15 us (2%)
    all_gather x3, waiting for transfers between devices, shards(): lax.all_gather(group_rows, 'dp', axis=0, tiled=True)  113 us
    all_gather x1, waiting for transfers between devices, shards(): lax.all_gather(second_rows, 'dp', axis=0, tiled=True)  102 us
    all_gather x1, waiting for transfers between devices, shards(): group_rows = lax.all_gather(inputs_first, 'seq', axis=0, tiled=True)  78.6 us
    all_gather x1, waiting for transfers between devices, shards(): second_rows = lax.all_gather(inputs_second, 'seq', axis=0, tiled=True)  74.8 us
    all_gather x1, waiting for transfers between devices, shards(): group_rows = lax.all_gather(output_first, 'seq', axis=0, tiled=True)  66.6 us
    all_gather x1, waiting for transfers between devices, shards(): group_rows = lax.all_gather(output_second, 'seq', axis=0, tiled=True)  62 us
    dot_general x4, matrix products, accumulate(): return jnp.dot(hidden, block_rows, preferred_element_type=jnp.float32)  32.4 us
    all_to_all x1, waiting for transfers between devices, shards(): lax.all_to_all(queries, 'seq', split_axis=1, concat_axis=0, tiled=True)  19.6 us
  transfers between devices with their start and end apart: 12, of which 10 were waited for; matrix products, arithmetic and copies ran while one was open for 13% of the time, Pallas kernels for 0%

commit v1 on v0

--- a/solution.py
+++ b/solution.py
@@ -87,7 +87,10 @@
 
 def columns_then_back(triple):
     attended = column_attention(triple[0], triple[1], triple[2])
-    return lax.all_to_all(attended, "seq", split_axis=0, concat_axis=1, tiled=True)
+    return jnp.concatenate(
+        lax.all_to_all(jnp.stack(jnp.split(attended, lax.axis_size("seq"), axis=0)), "seq", 0, 0),
+        axis=1,
+    )
 
 
 def accumulate(hidden, block_rows):

time: 712 us -> 694 us (0.975)
  waiting for transfers between devices: 569 us -> 528 us
  local copies, waits for them, and re-layouts: 36.2 us -> 56.3 us
    all_gather x1, waiting for transfers between devices: 62 us -> 40 us  [shards(): group_rows = lax.all_gather(output_second, 'seq', axis=0, tiled=True)]
    all_gather x3, waiting for transfers between devices: 113 us -> 132 us  [shards(): lax.all_gather(group_rows, 'dp', axis=0, tiled=True)]
    unnamed x16 -> x47, local copies, waits for them, and re-layouts: 2.06 us -> 20.9 us
    all_to_all x1, waiting for transfers between devices: 17.5 us -> 0.01 us  [columns_then_back(): lax.all_to_all(jnp.stack(jnp.split(attended, lax.axis_size('seq'), axis=0...]
    all_to_all x1, waiting for transfers between devices: 14.7 us -> 0.01 us  [shards(): lax.all_to_all(values, 'seq', split_axis=1, concat_axis=0, tiled=True)]
  transfers between devices with their start and end apart: 12 -> 12, of which waited for: 10 -> 9; matrix products, arithmetic and copies ran while one was open for 13% -> 15% of each run, Pallas kernels for 0% -> 0%
where the time goes in v1:
time: 694 us; the launch traced here: 691 us
  waiting for transfers between devices  528 us (76%)
  matrix products  59.2 us (9%)
  local copies, waits for them, and re-layouts  56.3 us (8%)
  starting transfers between devices  25.4 us (4%)
  between operations  14.9 us (2%)
    all_gather x3, waiting for transfers between devices, shards(): lax.all_gather(group_rows, 'dp', axis=0, tiled=True)  132 us
    all_gather x1, waiting for transfers between devices, shards(): lax.all_gather(second_rows, 'dp', axis=0, tiled=True)  102 us
    all_gather x1, waiting for transfers between devices, shards(): group_rows = lax.all_gather(inputs_first, 'seq', axis=0, tiled=True)  79.1 us
    all_gather x1, waiting for transfers between devices, shards(): second_rows = lax.all_gather(inputs_second, 'seq', axis=0, tiled=True)  74.8 us
    all_gather x1, waiting for transfers between devices, shards(): group_rows = lax.all_gather(output_first, 'seq', axis=0, tiled=True)  66.6 us
    all_gather x1, waiting for transfers between devices, shards(): group_rows = lax.all_gather(output_second, 'seq', axis=0, tiled=True)  40 us
    dot_general x4, matrix products, accumulate(): return jnp.dot(hidden, block_rows, preferred_element_type=jnp.float32)  32.4 us
    unnamed x47, local copies, waits for them, and re-layouts  20.9 us
  transfers between devices with their start and end apart: 12, of which 9 were waited for; matrix products, arithmetic and copies ran while one was open for 15% of the time, Pallas kernels for 0%

profile of v1, /device:TPU:0, one launch (start us, length us, event | category | flops | bytes accessed | tf_op | source)
XLA Modules:
  0.0 690.8 jit_solution(8074580312568889385)
XLA Ops:
  6.5 0.7 all-gather.9.cloned.1.call-update
  7.3 0.7 all-gather.13.cloned.1.call-update
  8.1 0.7 all-gather.17.cloned.1.call-update
  8.8 79.1 %all-gather.9.cloned.1.call-done = bf16[512,3072]{1,0:T(8,128)(2,1)} async-done(((bf16[16,3072]{1,0:T(8,128)(2,1)}), bf16[512,3072]{1,0:T(8,128)(2,1)}) %all-gather.9.cloned.1.call-update) | async-done | bytes 3145744 | tf_op jit(solution)/shard_map/all_gather | solution.py:120
  88.0 66.6 %all-gather.13.cloned.1.call-done = bf16[256,2048]{1,0:T(8,128)(2,1)} async-done(((bf16[8,2048]{1,0:T(8,128)(2,1)}), bf16[256,2048]{1,0:T(8,128)(2,1)}) %all-gather.13.cloned.1.call-update) | async-done | bytes 1048592 | tf_op jit(solution)/shard_map/all_gather | solution.py:127
  154.7 74.8 %all-gather.17.cloned.1.call-done = bf16[512,3072]{1,0:T(8,128)(2,1)} async-done(((bf16[16,3072]{1,0:T(8,128)(2,1)}), bf16[512,3072]{1,0:T(8,128)(2,1)}) %all-gather.17.cloned.1.call-update) | async-done | bytes 3145744 | tf_op jit(solution)/shard_map/all_gather | solution.py:131
  233.6 108.9 %all-gather.11.cloned.1.call-done = bf16[2048,3072]{1,0:T(8,128)(2,1)} async-done(((bf16[512,3072]{1,0:T(8,128)(2,1)}), bf16[2048,3072]{1,0:T(8,128)(2,1)}) %all-gather.11.cloned.1.call-update) | async-done | bytes 12582928 | tf_op jit(solution)/shard_map/all_gather | solution.py:121
  342.6 16.8 %copy.918 = bf16[3072,2048]{1,0:T(8,128)(2,1)} copy(bf16[3072,2048]{0,1:T(8,128)(2,1)} %bitcast.161) | data formatting | bytes 25165824 | tf_op jit(solution)/shard_map/dot_general | solution.py:97
  359.4 9.6 %convolution_bitcast_fusion = f32[1,512,3,8,128]{1,4,3,2,0:T(8,128)S(1)} fusion(bf16[3,8,128,2048]{3,2,1,0:T(8,128)(2,1)} %bitcast.162, bf16[1,512,2048]{2,1,0:T(8,128)(2,1)S(1)} %copy-done.3, f32[2048]{0:T(1024)S(1)} %copy-done.5, f32[512]{0:T(512)S(1)} %add_rsqrt_fusion.1), kind=kOutput, calls=%fused_computation.34 | convolution fusion | flops 6446645248 | bytes 20981760 | tf_op jit(solution)/shard_map/dot_general | solution.py:97
  369.5 0.7 subtract_convert_fusion.2
  370.2 1.5 maximum_bitcast_fusion
  371.7 1.1 fusion.33
  372.8 28.9 %while.10 = (s32[]{:T(128)}, bf16[8,512,128]{1,2,0:T(8,128)(2,1)}, bf16[8,512,128]{1,2,0:T(8,128)(2,1)}, bf16[8,512,128]{1,2,0:T(8,128)(2,1)}, bf16[8,512,128]{1,2,0:T(8,128)(2,1)}, /*index=5*/s32[]{:T(128)}) while((s32[]{:T(128)}, bf16[8,512,128]{1,2,0:T(8,128)(2,1)}, bf16[8,512,128]{1,2,0:T(8,128)(2,1)}, bf16[8,512,128]{1,2,0:T(8,128)(2,1)}, ...), condition=%wide.region_4.5_spmd, body=%wide.region_1.4_spmd.sunk | while | flops 136641536 | bytes 4206661 | solution.py:69
  372.8 1.3 fusion.80
  374.4 1.3 fusion.82
  375.8 0.7 constant_dynamic-update-slice_fusion.34
  376.4 1.3 fusion.80
  378.0 1.3 fusion.82
  379.4 0.7 constant_dynamic-update-slice_fusion.34
  380.1 1.3 fusion.80
  381.6 1.3 fusion.82
  383.0 0.7 constant_dynamic-update-slice_fusion.34
  383.7 1.3 fusion.80
  385.2 1.3 fusion.82
  386.6 0.7 constant_dynamic-update-slice_fusion.34
  387.3 1.3 fusion.80
  388.8 1.3 fusion.82
  390.2 0.7 constant_dynamic-update-slice_fusion.34
  390.9 1.3 fusion.80
  392.4 1.3 fusion.82
  393.8 0.7 constant_dynamic-update-slice_fusion.34
  394.5 1.3 fusion.80
  396.0 1.3 fusion.82
  397.4 0.7 constant_dynamic-update-slice_fusion.34
  398.1 1.3 fusion.80
  399.6 1.3 fusion.82
  401.1 0.7 constant_dynamic-update-slice_fusion.34
  401.7 6.6 fusion.18
  408.3 101.9 %all-gather.19.cloned.1.call-done = bf16[2048,3072]{1,0:T(8,128)(2,1)} async-done(((bf16[512,3072]{1,0:T(8,128)(2,1)}), bf16[2048,3072]{1,0:T(8,128)(2,1)}) %all-gather.19.cloned.1.call-update) | async-done | bytes 12582928 | tf_op jit(solution)/shard_map/all_gather | solution.py:132
  510.2 10.3 %fusion.23 = f32[512,3072]{0,1:T(8,128)S(1)} fusion(bf16[2048,3072]{1,0:T(8,128)(2,1)} %all-gather.19.cloned.1.call-done, bf16[512,2048]{1,0:T(8,128)(2,1)} %get-tuple-element.263, f32[2048]{0:T(1024)S(1)} %copy-done.6, f32[512]{0:T(512)S(1)} %add_rsqrt_fusion), kind=kOutput, calls=%fused_computation.35 | convolution fusion | flops 6446645248 | bytes 20981760 | tf_op jit(solution)/shard_map/dot_general | solution.py:97
  521.2 2.0 copy-done.2
  523.2 0.7 subtract_convert_fusion.1
  524.1 1.5 copy.925
  525.5 9.8 %all-to-all-start.1 = ((bf16[1,512,8,128]{3,2,0,1:T(8,128)(2,1)}), bf16[1,512,8,128]{3,2,0,1:T(8,128)(2,1)S(1)}, u32[]{:S(2)}, u32[]{:S(2)}) async-start(bf16[1,512,8,128]{3,2,0,1:T(8,128)(2,1)} %copy.925), calls=%async_computation.1 | async-start | bytes 2097152 | tf_op jit(solution)/shard_map/all_to_all | solution.py:140
  535.4 0.7 all-gather.21.cloned.1.call-update
  536.2 1.5 copy.926
  537.7 15.9 %all-to-all-done.1 = bf16[1,512,8,128]{3,2,0,1:T(8,128)(2,1)S(1)} async-done(((bf16[1,512,8,128]{3,2,0,1:T(8,128)(2,1)}), bf16[1,512,8,128]{3,2,0,1:T(8,128)(2,1)S(1)}, u32[]{:S(2)}, u32[]{:S(2)}) %all-to-all-start.1) | async-done | bytes 1048608 | tf_op jit(solution)/shard_map/all_to_all | solution.py:140
  553.6 6.0 all-to-all-start.2
  559.6 1.7 fusion.34
  561.3 1.5 copy.924
  562.8 14.8 %all-to-all-done.2 = bf16[1,512,8,128]{3,2,0,1:T(8,128)(2,1)S(1)} async-done(((bf16[1,512,8,128]{3,2,0,1:T(8,128)(2,1)}), bf16[1,512,8,128]{3,2,0,1:T(8,128)(2,1)S(1)}, u32[]{:S(2)}, u32[]{:S(2)}) %all-to-all-start.2) | async-done | bytes 1048608 | tf_op jit(solution)/shard_map/all_to_all | solution.py:141
  577.7 4.7 all-to-all-start
  582.4 40.0 %all-gather.21.cloned.1.call-done = bf16[256,2048]{1,0:T(8,128)(2,1)} async-done(((bf16[8,2048]{1,0:T(8,128)(2,1)}), bf16[256,2048]{1,0:T(8,128)(2,1)}) %all-gather.21.cloned.1.call-update) | async-done | bytes 1048592 | tf_op jit(solution)/shard_map/all_gather | solution.py:146
  622.4 3.3 fusion.65
  625.6 2.6 fusion.32
  628.2 0.9 fusion.63
  637.0 1.3 fusion.62
  644.4 0.6 constant_dynamic-update-slice_fusion.9
  646.3 0.6 constant_dynamic-update-slice_fusion.6
  648.1 0.6 constant_dynamic-update-slice_fusion.3
  649.3 0.6 constant_dynamic-update-slice_fusion.1
  650.0 4.6 all-to-all-start.3
  654.6 23.5 %all-gather.23.cloned.1.call-done = bf16[1024,2048]{1,0:T(8,128)(2,1)} async-done(((bf16[256,2048]{1,0:T(8,128)(2,1)}), bf16[1024,2048]{1,0:T(8,128)(2,1)}) %all-gather.23.cloned.1.call-update) | async-done | bytes 4194320 | tf_op jit(solution)/shard_map/all_gather | solution.py:147
  678.1 5.9 fusion.22
  (88 shorter events, 24.0 us)
Async XLA Ops:
  6.5 224.9 %copy-start = (s32[1,32]{1,0:T(1,128)S(1)}, s32[1,32]{1,0:T(1,128)}, u32[]{:S(2)}) copy-start(s32[1,32]{1,0:T(1,128)} %param.18) | copy-start | bytes 388
  6.5 81.4 %all-gather.9.cloned.1.call-start = ((), (), s32[]{:S(2)}) async-start(), calls=%async_computation.4 | async-start | bytes 3244032 | tf_op jit(solution)/shard_map/all_gather | solution.py:120
  7.3 147.4 %all-gather.13.cloned.1.call-start = ((), (), s32[]{:S(2)}) async-start(), calls=%async_computation.6 | async-start | bytes 1081344 | tf_op jit(solution)/shard_map/all_gather | solution.py:127
  8.0 221.5 %all-gather.17.cloned.1.call-start = ((), (), s32[]{:S(2)}) async-start(), calls=%async_computation.8 | async-start | bytes 3244032 | tf_op jit(solution)/shard_map/all_gather | solution.py:131
  8.7 333.8 %all-gather.11.cloned.1.call-start = ((), (), s32[]{:S(2)}) async-start(), calls=%async_computation.5 | async-start | bytes 15728640 | tf_op jit(solution)/shard_map/all_gather | solution.py:121
  88.0 313.8 %all-gather.15.cloned.1.call-start = ((), (), s32[]{:S(2)}) async-start(), calls=%async_computation.7 | async-start | bytes 5242880 | tf_op jit(solution)/shard_map/all_gather | solution.py:128
  154.6 75.0 %copy-start.4 = (s32[2]{0:T(128)S(1)}, s32[2]{0:T(128)}, u32[]{:S(2)}) copy-start(s32[2]{0:T(128)} %param.19) | copy-start | bytes 28
  154.6 78.0 %copy-start.3 = (bf16[1,512,2048]{2,1,0:T(8,128)(2,1)S(1)}, bf16[1,512,2048]{2,1,0:T(8,128)(2,1)}, u32[]{:S(2)}) copy-start(bf16[1,512,2048]{2,1,0:T(8,128)(2,1)} %param.11) | copy-start | bytes 6291460
  154.7 355.6 %all-gather.19.cloned.1.call-start = ((), (), s32[]{:S(2)}) async-start(), calls=%async_computation.9 | async-start | bytes 15728640 | tf_op jit(solution)/shard_map/all_gather | solution.py:132
  342.6 16.8 %copy-start.5 = (f32[2048]{0:T(1024)S(1)}, f32[2048]{0:T(1024)}, u32[]{:S(2)}) copy-start(f32[2048]{0:T(1024)} %param.12) | copy-start | bytes 24580
  401.7 108.5 %copy-start.6 = (f32[2048]{0:T(1024)S(1)}, f32[2048]{0:T(1024)}, u32[]{:S(2)}) copy-start(f32[2048]{0:T(1024)} %param.15) | copy-start | bytes 24580
  520.6 2.7 copy-start.2
  525.5 28.0 %all-to-all-start.1 = ((bf16[1,512,8,128]{3,2,0,1:T(8,128)(2,1)}), bf16[1,512,8,128]{3,2,0,1:T(8,128)(2,1)S(1)}, u32[]{:S(2)}, u32[]{:S(2)}) async-start(bf16[1,512,8,128]{3,2,0,1:T(8,128)(2,1)} %copy.925), calls=%async_computation.1 | async-start | bytes 2097152 | tf_op jit(solution)/shard_map/all_to_all | solution.py:140
  535.4 87.0 %all-gather.21.cloned.1.call-start = ((), (), s32[]{:S(2)}) async-start(), calls=%async_computation.10 | async-start | bytes 1081344 | tf_op jit(solution)/shard_map/all_gather | solution.py:146
  553.6 24.1 %all-to-all-start.2 = ((bf16[1,512,8,128]{3,2,0,1:T(8,128)(2,1)}), bf16[1,512,8,128]{3,2,0,1:T(8,128)(2,1)S(1)}, u32[]{:S(2)}, u32[]{:S(2)}) async-start(bf16[1,512,8,128]{3,2,0,1:T(8,128)(2,1)} %copy.926), calls=%async_computation.2 | async-start | bytes 2097152 | tf_op jit(solution)/shard_map/all_to_all | solution.py:141
  577.7 48.0 %all-to-all-start = ((bf16[1,512,8,128]{3,2,0,1:T(8,128)(2,1)}), bf16[1,512,8,128]{3,2,0,1:T(8,128)(2,1)S(1)}, u32[]{:S(2)}, u32[]{:S(2)}) async-start(bf16[1,512,8,128]{3,2,0,1:T(8,128)(2,1)} %copy.924), calls=%async_computation | async-start | bytes 2097152 | tf_op jit(solution)/shard_map/all_to_all | solution.py:142
  582.3 95.7 %all-gather.23.cloned.1.call-start = ((), (), s32[]{:S(2)}) async-start(), calls=%async_computation.11 | async-start | bytes 5242880 | tf_op jit(solution)/shard_map/all_gather | solution.py:147
  638.4 39.7 %copy-start.7 = (bf16[512,2048]{1,0:T(8,128)(2,1)S(1)}, bf16[512,2048]{1,0:T(8,128)(2,1)}, u32[]{:S(2)}) copy-start(bf16[512,2048]{1,0:T(8,128)(2,1)} %get-tuple-element.263) | copy-start | bytes 6291460
  650.0 28.1 %all-to-all-start.3 = ((bf16[32,1,16,8,128]{4,3,2,1,0:T(8,128)(2,1)}), bf16[32,1,16,8,128]{4,3,2,1,0:T(8,128)(2,1)S(1)}, u32[]{:S(2)}, u32[]{:S(2)}) async-start(bf16[32,1,16,8,128]{4,3,2,1,0:T(8,128)(2,1)} %constant_dynamic-update-slice_fusion.1), calls=%async_computation.3 | async-start | bytes 2097152 | tf_op jit(solution)/shard_map/all_to_all | solution.py:91
  678.1 5.9 copy-start.1
Sparse Core Ops, SparseCore 0:
  10.4 77.4 all-gather.8
  90.9 63.6 all-gather.12
  157.7 71.8 all-gather.16
  231.1 111.4 all-gather.10
  344.1 48.7 all-gather.14
  394.4 115.8 all-gather.18
  539.2 83.0 all-gather.20
  624.0 54.0 all-gather.22
